TPU v7x, 32 devices: a whole 2x2x4 slice. The times are simulated.
32 devices in a mesh: dp: 4 (over z), row: 2 (over x), col: 4 (over y, core).
Axes of the slice: x: 2, y: 2, z: 4, core: 2. Of those that a mesh axis runs over, the one named last changes fastest.
Arguments:
- tokens: bfloat16 [768, 16384], P(('row', 'col'), 'dp'), may hold values from -6 to 6
- cotangent: bfloat16 [768, 16384], P(('row', 'col'), 'dp'), may hold values from -6 to 6
- holder_of: int32 [8, 4], replicated, may hold values from 0 to 3, each once within a row
- lengths: int32 [8, 4, 4], replicated, may hold values from 0 to 512, as said below
- input_gain: float32 [768], P(('row', 'col')), may hold values from 0.5 to 1.5
- input_shift: float32 [768], P(('row', 'col')), may hold values from -1.5 to 1.5
- attend_weight: bfloat16 [3, 768, 768], P(None, 'col', 'row'), may hold values from -0.21875 to 0.21875
- attend_bias: float32 [2, 768], P(None, 'col'), may hold values from -1.5 to 1.5
- mixed_gain: float32 [768], P('col'), may hold values from 0.5 to 1.5
- mixed_shift: float32 [768], P('col'), may hold values from -1.5 to 1.5
- output_weight: bfloat16 [768, 768], P('col', 'row'), may hold values from -0.375 to 0.375
- output_bias: float32 [768], P(('row', 'col')), may hold values from -1.5 to 1.5
- middle_gain: float32 [768], P(('row', 'col')), may hold values from 0.5 to 1.5
- middle_shift: float32 [768], P(('row', 'col')), may hold values from -1.5 to 1.5
- expand_weight: bfloat16 [768, 3072], P('row', 'col'), may hold values from -0.375 to 0.375
- expand_bias: float32 [3072], P('col'), may hold values from -1.5 to 1.5
- hidden_gain: float32 [3072], P('col'), may hold values from 0.5 to 1.5
- hidden_shift: float32 [3072], P('col'), may hold values from -1.5 to 1.5
- shrink_weight: bfloat16 [3072, 768], P('col', 'row'), may hold values from -0.1875 to 0.1875
- shrink_bias: float32 [768], P(('row', 'col')), may hold values from -1.5 to 1.5
Outputs:
- block_out: bfloat16 [768, 16384], P(('row', 'col'), 'dp')
- input_grad: bfloat16 [768, 16384], P(('row', 'col'), 'dp')
- input_gain_grad: float32 [768], P(('row', 'col'))
- input_shift_grad: float32 [768], P(('row', 'col'))
- attend_weight_grad: float32 [3, 768, 768], P(None, 'col', 'row')
- attend_bias_grad: float32 [2, 768], P(None, 'col')
- mixed_gain_grad: float32 [768], P('col')
- mixed_shift_grad: float32 [768], P('col')
- output_weight_grad: float32 [768, 768], P('col', 'row')
- output_bias_grad: float32 [768], P(('row', 'col'))
- middle_gain_grad: float32 [768], P(('row', 'col'))
- middle_shift_grad: float32 [768], P(('row', 'col'))
- expand_weight_grad: float32 [768, 3072], P('row', 'col')
- expand_bias_grad: float32 [3072], P('col')
- hidden_gain_grad: float32 [3072], P('col')
- hidden_shift_grad: float32 [3072], P('col')
- shrink_weight_grad: float32 [3072, 768], P('col', 'row')
- shrink_bias_grad: float32 [768], P(('row', 'col'))
Inputs may be any that keep to these rules, and one draw needn't show every extreme that they name: Each row of holder_of names every holder once. The 4 lengths of a unit add up to 512; a zero length is an empty slot; in every micro-batch one unit is a single sequence of 512 tokens.
All inputs are finite; a program needn't handle non-finite values.
Results may differ from a plain program's by a relative error of at most 0.017.
Values may be sent and summed in bfloat16 or wider, within the bound.
No kernel may reach another device: no remote copies, remote signals or barrier semaphores. Data moves between devices by JAX's collectives and lax.ppermute only.
A program may use at most 128 MiB of HBM per device.

v0:
```python
import math
import jax
import jax.numpy as jnp
from jax import lax
from jax.sharding import PartitionSpec as P

HEAD = 64
eps = 1e-05
masked_score = -1e30
f32 = jnp.float32
bf16 = jnp.bfloat16
RC = ("row", "col")


def mm(spec, a, b):
    return jnp.einsum(spec, a, b, preferred_element_type=f32)


def norm(v, gain, shift):
    mu = jnp.mean(v, axis=0, keepdims=True)
    d = v - mu
    r = lax.rsqrt(jnp.mean(d * d, axis=0, keepdims=True) + eps)
    vh = d * r
    return (vh * gain + shift, vh, r)


def norm_back(up, vh, r, gain):
    h = up * gain
    m1 = jnp.mean(h, axis=0, keepdims=True)
    m2 = jnp.mean(h * vh, axis=0, keepdims=True)
    return (
        r * (h - m1 - vh * m2),
        jnp.sum(up * vh, axis=1, keepdims=True),
        jnp.sum(up, axis=1, keepdims=True),
    )


def scores_of(q, k, visible):
    s = mm("hek,heq->hkq", k, q) * (1.0 / math.sqrt(HEAD))
    return jnp.where(visible[None], s, masked_score)


def body(
    tokens,
    cotangent,
    holder_of,
    lengths,
    input_gain,
    input_shift,
    attend_weight,
    attend_bias,
    mixed_gain,
    mixed_shift,
    output_weight,
    output_bias,
    middle_gain,
    middle_shift,
    expand_weight,
    expand_bias,
    hidden_gain,
    hidden_shift,
    shrink_weight,
    shrink_bias,
):
    holders = lax.axis_size("dp")
    half = holders // 2
    nr, nc = (lax.axis_size("row"), lax.axis_size("col"))
    n = nr * nc
    micro = holder_of.shape[0]
    assert micro == n
    fl = tokens.shape[0]
    pairs = micro * half
    blk = tokens.shape[1] // pairs
    unit = half * blk
    dp = lax.axis_index("dp")
    side, pos = (dp // half, dp % half)
    rc = lax.axis_index("row") * nc + lax.axis_index("col")
    groups = [[s * half + p for p in range(half)] for s in range(2)]

    def to_unit(v):
        v = v.reshape(fl, half, n, blk)
        v = jnp.transpose(v, (1, 2, 0, 3))
        v = lax.all_to_all(v, "dp", 0, 0, axis_index_groups=groups, tiled=True)
        v = jnp.transpose(v, (1, 2, 0, 3)).reshape(n, fl, unit)
        v = lax.all_to_all(v, RC, 0, 0, tiled=True)
        return v.reshape(n * fl, unit)

    def from_unit(v):
        v = lax.all_to_all(v.reshape(n, fl, unit), RC, 0, 0, tiled=True)
        v = jnp.transpose(v.reshape(n, fl, half, blk), (2, 0, 1, 3))
        v = lax.all_to_all(v, "dp", 0, 0, axis_index_groups=groups, tiled=True)
        return jnp.transpose(v, (2, 0, 1, 3)).reshape(tokens.shape)

    def gather(v):
        return lax.all_gather(v, RC, axis=0)

    ga = gather(attend_weight)
    go = gather(output_weight)
    ge = gather(expand_weight)
    gs = gather(shrink_weight)
    hw, rw, fw = (output_weight.shape[0], output_weight.shape[1], shrink_weight.shape[0])
    thin = jnp.concatenate(
        [
            v.reshape(-1)
            for v in (
                input_gain,
                input_shift,
                output_bias,
                middle_gain,
                middle_shift,
                shrink_bias,
                attend_bias,
                mixed_gain,
                mixed_shift,
                expand_bias,
                hidden_gain,
                hidden_shift,
            )
        ]
    )
    thin = lax.all_gather(thin, RC, axis=0)
    sizes = [fl] * 6 + [hw] * 4 + [fw] * 3
    cols, at = ([], 0)
    for i, size in enumerate(sizes):
        piece = thin[:, at : at + size] if i < 6 else thin[:nc, at : at + size]
        cols.append(piece.reshape(-1, 1))
        at += size
    in_g, in_s, out_b, mid_g, mid_s, shr_b, q_b, v_b, mix_g, mix_s, exp_b, hid_g, hid_s = cols
    k_unit = 2 * (pos * n + rc) + side
    m_of, u_of = (k_unit // holders, k_unit % holders)
    own = lengths[m_of, holder_of[m_of, u_of]]
    bounds = jnp.cumsum(own)[:-1]
    at_row = jnp.arange(unit, dtype=jnp.int32)
    segment = jnp.sum((at_row[:, None] >= bounds[None, :]).astype(jnp.int32), axis=1)
    visible = segment[:, None] == segment[None, :]
    x = to_unit(tokens).astype(f32)
    e2 = to_unit(cotangent)
    a, vh_in, r_in = norm(x, in_g, in_s)
    a = a.astype(bf16)
    gar = ga.reshape(nr, nc, 3, hw, rw)
    trip = mm("rcjif,rft->jcit", gar, a.reshape(nr, rw, unit)).reshape(3, nc * hw, unit)
    heads = lambda v: v.reshape(-1, HEAD, unit)
    q = heads((trip[0] + q_b).astype(bf16))
    k = heads(trip[1].astype(bf16))
    v = heads((trip[2] + v_b).astype(bf16))
    s = scores_of(q, k, visible)
    top = jnp.max(s, axis=1, keepdims=True)
    ex = jnp.exp(s - top)
    den = jnp.sum(ex, axis=1, keepdims=True)
    prob = ex / den
    o = mm("hek,hkq->heq", v, prob.astype(bf16)).reshape(nc * hw, unit)
    on, vh_mix, r_mix = norm(o, mix_g, mix_s)
    on = on.astype(bf16)
    gor = go.reshape(nr, nc * hw, rw)
    x1 = x + mm("rin,it->rnt", gor, on).reshape(nr * rw, unit) + out_b
    b, vh_mid, r_mid = norm(x1, mid_g, mid_s)
    b = b.astype(bf16)
    ger = ge.reshape(nr, nc, rw, fw)
    f = mm("rckn,rkt->cnt", ger, b.reshape(nr, rw, unit)).reshape(nc * fw, unit) + exp_b
    phi = 0.5 * (1.0 + lax.erf(f * math.sqrt(0.5)))
    g = f * phi
    gn, vh_hid, r_hid = norm(g, hid_g, hid_s)
    gn = gn.astype(bf16)
    gsr = gs.reshape(nr, nc * fw, rw)
    y = x1 + mm("rfn,ft->rnt", gsr, gn).reshape(nr * rw, unit) + shr_b
    block_out = from_unit(y.astype(bf16))
    e2r = e2.reshape(nr, rw, unit)
    d_shr_w = mm("cft,rdt->rcfd", gn.reshape(nc, fw, unit), e2r).astype(bf16)
    dy = e2.astype(f32)
    d_shr_b = jnp.sum(dy, axis=1, keepdims=True)
    dgn = mm("rfd,rdt->ft", gsr, e2r)
    dg, d_hid_g, d_hid_s = norm_back(dgn, vh_hid, r_hid, hid_g)
    slope = phi + f * (jnp.exp(-0.5 * f * f) * (1.0 / math.sqrt(2.0 * math.pi)))
    df = (dg * slope).astype(bf16)
    d_exp_b = jnp.sum(df.astype(f32), axis=1, keepdims=True)
    dfc = df.reshape(nc, fw, unit)
    d_exp_w = mm("rkt,cnt->rckn", b.reshape(nr, rw, unit), dfc).astype(bf16)
    db = mm("rckn,cnt->rkt", ger, dfc).reshape(nr * rw, unit)
    dx1, d_mid_g, d_mid_s = norm_back(db, vh_mid, r_mid, mid_g)
    dx1 = dy + dx1
    e1 = dx1.astype(bf16)
    d_out_b = jnp.sum(e1.astype(f32), axis=1, keepdims=True)
    e1r = e1.reshape(nr, rw, unit)
    d_out_w = mm("cit,rnt->rcin", on.reshape(nc, hw, unit), e1r).astype(bf16)
    don = mm("rin,rnt->it", gor, e1r)
    do, d_mix_g, d_mix_s = norm_back(don, vh_mix, r_mix, mix_g)
    do = heads(do.astype(bf16))
    dprob = mm("hek,heq->hkq", v, do)
    inner = jnp.sum(prob * dprob, axis=1, keepdims=True)
    ds = (prob * (dprob - inner)).astype(bf16)
    scale = 1.0 / math.sqrt(HEAD)
    dq = (mm("hek,hkq->heq", k, ds) * scale).astype(bf16).reshape(nc, hw, unit)
    dk = (mm("heq,hkq->hek", q, ds) * scale).astype(bf16).reshape(nc, hw, unit)
    dv = mm("heq,hkq->hek", do, prob.astype(bf16)).astype(bf16).reshape(nc, hw, unit)
    d_q_b = jnp.sum(dq.astype(f32), axis=2)
    d_v_b = jnp.sum(dv.astype(f32), axis=2)
    dtrip = jnp.stack([dq, dk, dv], axis=1)
    d_att_w = mm("cjit,rft->rcjif", dtrip, a.reshape(nr, rw, unit)).astype(bf16)
    da = mm("rcjif,cjit->rft", gar, dtrip).reshape(nr * rw, unit)
    dx, d_in_g, d_in_s = norm_back(da, vh_in, r_in, in_g)
    input_grad = from_unit((dx1 + dx).astype(bf16))

    def reduce(v):
        v = v.reshape((n,) + v.shape[2:])
        return lax.psum(lax.psum_scatter(v, RC, scatter_dimension=0, tiled=False), "dp")

    shr_w_g = reduce(d_shr_w).astype(f32)
    exp_w_g = reduce(d_exp_w).astype(f32)
    out_w_g = reduce(d_out_w).astype(f32)
    by_rc = [v.reshape(n, fl) for v in (d_in_g, d_in_s, d_out_b, d_mid_g, d_mid_s, d_shr_b)]
    by_c = [
        jnp.broadcast_to(v.reshape(1, nc, -1), (nr, nc, v.size // nc)).reshape(n, -1)
        for v in (d_q_b, d_v_b, d_mix_g, d_mix_s, d_exp_b, d_hid_g, d_hid_s)
    ]
    small = jnp.concatenate(by_rc + by_c, axis=1).astype(bf16)
    width = small.shape[1]
    pad = -width % rw
    small = jnp.pad(small, ((0, 0), (0, pad))).reshape(nr, nc, -1, rw)
    last = jnp.concatenate([d_att_w.reshape(nr, nc, 3 * hw, rw), small], axis=2)
    last = reduce(last).astype(f32)
    att_w_g = last[: 3 * hw].reshape(attend_weight.shape)
    flat = last[3 * hw :].reshape(-1)
    outs, at = ([], 0)
    for size in sizes:
        outs.append(flat[at : at + size])
        at += size
    (
        in_g_g,
        in_s_g,
        out_b_g,
        mid_g_g,
        mid_s_g,
        shr_b_g,
        q_b_g,
        v_b_g,
        mix_g_g,
        mix_s_g,
        exp_b_g,
        hid_g_g,
        hid_s_g,
    ) = outs
    return (
        block_out,
        input_grad,
        in_g_g,
        in_s_g,
        att_w_g,
        jnp.stack([q_b_g, v_b_g]),
        mix_g_g,
        mix_s_g,
        out_w_g,
        out_b_g,
        mid_g_g,
        mid_s_g,
        exp_w_g,
        exp_b_g,
        hid_g_g,
        hid_s_g,
        shr_w_g,
        shr_b_g,
    )


def solution(mesh):
    wide, narrow = (P(RC), P("col"))
    in_specs = (
        P(RC, "dp"),
        P(RC, "dp"),
        P(),
        P(),
        wide,
        wide,
        P(None, "col", "row"),
        P(None, "col"),
        narrow,
        narrow,
        P("col", "row"),
        wide,
        wide,
        wide,
        P("row", "col"),
        narrow,
        narrow,
        narrow,
        P("col", "row"),
        wide,
    )
    out_specs = (
        P(RC, "dp"),
        P(RC, "dp"),
        wide,
        wide,
        P(None, "col", "row"),
        P(None, "col"),
        narrow,
        narrow,
        P("col", "row"),
        wide,
        wide,
        wide,
        P("row", "col"),
        narrow,
        narrow,
        narrow,
        P("col", "row"),
        wide,
    )
    return jax.shard_map(body, mesh=mesh, in_specs=in_specs, out_specs=out_specs, check_vma=False)
```

profile of v0, /device:TPU:0, one launch (start us, length us, event | category | flops | bytes accessed | tf_op | source)
XLA Modules:
  0.0 607.2 jit_solution(13611442720965010342)
XLA Ops:
  15.2 4.3 all-to-all-start
  20.6 10.5 %all-to-all-done = bf16[2,8,96,256]{3,1,2,0:T(8,128)(2,1)S(1)} async-done(((bf16[2,8,96,256]{3,1,2,0:T(8,128)(2,1)}), bf16[2,8,96,256]{3,1,2,0:T(8,128)(2,1)S(1)}, u32[]{:S(2)}, u32[]{:S(2)}) %all-to-all-start) | async-done | bytes 786464 | tf_op jit(solution)/shard_map/all_to_all | solution.py:83
  31.1 3.5 all-to-all-start.4
  41.1 4.0 all-to-all-done.4
  45.1 3.5 all-to-all-start.1
  48.9 18.1 %all-reduce.6.cloned.1.call-done = f32[29184]{0:T(1024)} async-done(((f32[29184]{0:T(1024)}), f32[29184]{0:T(1024)}) %all-reduce.6.cloned.1.call-update) | async-done | bytes 116752
  73.3 4.2 all-to-all-start.5
  78.7 32.7 %all-gather.10.cloned.1.call-done = bf16[24,192,384]{2,1,0:T(8,128)(2,1)} async-done(((bf16[3,192,384]{2,1,0:T(8,128)(2,1)}), bf16[24,192,384]{2,1,0:T(8,128)(2,1)}) %all-gather.10.cloned.1.call-update) | async-done | bytes 3538960 | tf_op jit(solution)/shard_map/all_gather | solution.py:95
  111.5 4.1 convolution_bitcast_fusion.1
  117.9 10.7 %fusion.64 = (f32[12,512]{1,0:T(8,128)S(1)}, f32[12,512,512]{2,1,0:T(8,128)}) fusion(pred[512,512]{1,0:T(8,128)(4,1)S(1)} %broadcast_compare_fusion, bf16[12,64,512]{2,1,0:T(8,128)(2,1)S(1)} %bitcast.299, f32[12,64,512]{2,1,0:T(8,128)} %bitcast.302, f32[12,64]{1,0:T(8,128)S(1)} %add.260), kind=kOutput, calls=%fused_computation.139 | convolution fusion | flops 416023040 | bytes 15232000 | tf_op jit(solution)/shard_map/sub | solution.py:148
  128.6 6.6 %fusion.65 = (f32[512]{0:T(512)S(1)}, f32[12,64,512]{2,1,0:T(8,128)S(1)}) fusion(f32[12,512,512]{2,1,0:T(8,128)} %get-tuple-element.76, f32[12,512]{1,0:T(8,128)S(1)} %get-tuple-element.75, f32[12,64,512]{2,1,0:T(8,128)} %bitcast.321, f32[12,64]{1,0:T(8,128)S(1)} %add.249), kind=kOutput, calls=%fused_computation.140 | convolution fusion | flops 410123776 | bytes 15758336 | tf_op jit(solution)/shard_map/hek,hkq->heq/dot_general | solution.py:16
  138.3 2.3 fusion.68
  144.4 34.1 %all-gather.14.cloned.1.call-done = bf16[3072,768]{1,0:T(8,128)(2,1)} async-done(((bf16[384,768]{1,0:T(8,128)(2,1)}), bf16[3072,768]{1,0:T(8,128)(2,1)}) %all-gather.14.cloned.1.call-update) | async-done | bytes 4718608 | tf_op jit(solution)/shard_map/all_gather | solution.py:95
  178.5 9.2 %fusion.54 = (f32[512]{0:T(512)S(1)}, f32[4,768,512]{1,2,0:T(8,128)}, f32[4,768,512]{1,2,0:T(8,128)}) fusion(f32[4,768]{1,0:T(4,128)S(1)} %get-tuple-element.57, bf16[2,4,384,768]{3,2,1,0:T(8,128)(2,1)} %bitcast.344, f32[2,384]{1,0:T(2,128)S(1)} %add.275, f32[2,384]{1,0:T(2,128)S(1)} %mul.381, f32[512]{0:T(512)S(1)} %add_rsqrt_fusion.1, ...), kind=kOutput, calls=%fused_computation.130 | convolution fusion | flops 2427321856 | bytes 18898944 | tf_op jit(solution)/shard_map/rckn,rkt->cnt/dot_general | solution.py:16
  187.7 6.7 %copy.132 = f32[4,768,512]{2,1,0:T(8,128)} copy(f32[4,768,512]{1,2,0:T(8,128)} %get-tuple-element.79) | data formatting | bytes 12582912 | tf_op jit(solution)/shard_map/rckn,rkt->cnt/dot_general | solution.py:16
  194.3 3.5 multiply_reduce_fusion.2
  197.9 21.4 %all-gather.16.cloned.1.call-done = bf16[6144,384]{1,0:T(8,128)(2,1)} async-done(((bf16[768,384]{1,0:T(8,128)(2,1)}), bf16[6144,384]{1,0:T(8,128)(2,1)}) %all-gather.16.cloned.1.call-update) | async-done | bytes 4718608 | tf_op jit(solution)/shard_map/all_gather | solution.py:95
  219.3 8.5 %fusion.8 = (bf16[3072]{0:T(1024)(128)(2,1)S(1)}, f32[512]{0:T(512)S(1)}, f32[512]{0:T(512)S(1)}, bf16[3072]{0:T(1024)(128)(2,1)S(1)}, f32[3072,512,1]{1,0,2:T(8,128)S(1)}) fusion(f32[4,768,512]{2,1,0:T(8,128)} %copy.132, f32[512]{0:T(512)S(1)} %broadcast_multiply_fusion.2, f32[3072]{0:T(1024)S(1)} %add.288, f32[512]{0:T(512)S(1)} %add_rsqrt_fusion, ...), kind=kOutput, calls=%fused_computation.17 | convolution fusion | flops 2437932032 | bytes 18132992 | tf_op jit(solution)/shard_map/rfd,rdt->ft/dot_general | solution.py:16
  227.9 7.7 %fusion.52 = (bf16[3072]{0:T(1024)(128)(2,1)S(1)}, bf16[3072,512]{1,0:T(8,128)(2,1)S(1)}) fusion(f32[512]{0:T(512)S(1)} %get-tuple-element.89, f32[512]{0:T(512)S(1)} %broadcast_multiply_fusion.2, f32[3072]{0:T(1024)S(1)} %add.288, f32[4,768,512]{2,1,0:T(8,128)S(1)} %bitcast.285, f32[512]{0:T(512)S(1)} %get-tuple-element.90, f32[3072]{0:T(1024)S(1)} %mul.396, ...), kind=kLoop, calls=%fused_computation.129 | loop fusion | flops 31454208 | bytes 15767552 | tf_op jit(solution)/shard_map/reduce_sum | solution.py:175
  235.6 6.0 fusion.30
  241.7 2.2 add_convert_fusion.2
  247.0 2.3 copy.135
  249.3 7.9 %fusion.67 = (bf16[12,64]{1,0:T(8,128)(2,1)S(1)}, bf16[12,64,512]{2,1,0:T(8,128)(2,1)}) fusion(bf16[12,64,512]{2,1,0:T(8,128)(2,1)} %bitcast.331, f32[12,512,512]{2,1,0:T(8,128)} %get-tuple-element.76, f32[12,512]{1,0:T(8,128)S(1)} %get-tuple-element.75), kind=kOutput, calls=%fused_computation.142 | convolution fusion | flops 409730304 | bytes 14181888 | tf_op jit(solution)/shard_map/heq,hkq->hek/dot_general | solution.py:16
  257.2 8.9 %multiply_reduce_fusion = (f32[12,512]{1,0:T(8,128)S(1)}, f32[12,512,512]{2,1,0:T(8,128)}) fusion(f32[12,512,512]{2,1,0:T(8,128)} %get-tuple-element.76, f32[12,512]{1,0:T(8,128)S(1)} %get-tuple-element.75, bf16[12,64,512]{2,1,0:T(8,128)(2,1)S(1)} %bitcast.332, f32[12,64,512]{2,1,0:T(8,128)S(1)} %bitcast.322, f32[12,64]{1,0:T(8,128)S(1)} %add.249), kind=kOutput, calls=%fused_computation.2 | convolution fusion | flops 412870656 | bytes 27577344 | tf_op jit(solution)/shard_map/hek,heq->hkq/dot_general | solution.py:16
  266.1 6.5 %multiply_convert_fusion = bf16[12,512,512]{2,1,0:T(8,128)(2,1)S(1)} fusion(f32[12,512,512]{2,1,0:T(8,128)} %get-tuple-element.84, f32[12,512]{1,0:T(8,128)S(1)} %get-tuple-element.83, f32[12,512,512]{2,1,0:T(8,128)S(1)} %bitcast.298, f32[12,512]{1,0:T(8,128)S(1)} %get-tuple-element.75), kind=kLoop, calls=%fused_computation.1 | loop fusion | flops 12582912 | bytes 31506432 | tf_op jit(solution)/shard_map/convert_element_type | solution.py:190
  272.7 2.9 multiply_convert_fusion.1
  279.4 6.0 fusion.22
  286.3 2.2 fusion.24
  288.8 3.6 fusion.51
  292.6 4.0 convolution_convert_fusion
  299.5 4.0 add_convert_fusion
  305.2 4.2 convert_bitcast_fusion
  309.4 2.6 copy.145
  313.4 7.2 %convert_bitcast_fusion.1 = bf16[2,4,384,768]{2,3,0,1:T(8,128)(2,1)} fusion(bf16[4,768,512,1]{2,1,3,0:T(8,128)(2,1)} %bitcast.317, f32[2,384,512]{2,1,0:T(8,128)S(1)} %copy-done.10, f32[2,384]{1,0:T(2,128)S(1)} %add.275, f32[2,384]{1,0:T(2,128)S(1)} %mul.381, f32[512]{0:T(512)S(1)} %add_rsqrt_fusion.1, f32[512]{0:T(512)S(1)} %broadcast_multiply_fusion.9), kind=kOutput, calls=%fused_computation.30 | convolution fusion | flops 2420244480 | bytes 9447424 | tf_op jit(solution)/shard_map/rkt,cnt->rckn/dot_general | solution.py:16
  320.7 6.7 %copy.143 = bf16[2,4,384,768]{3,2,1,0:T(8,128)(2,1)} copy(bf16[2,4,384,768]{2,3,0,1:T(8,128)(2,1)} %convert_bitcast_fusion.1) | data formatting | bytes 9437184 | tf_op jit(solution)/shard_map/convert_element_type | solution.py:177
  327.4 4.8 copy.126
  332.2 5.8 fusion.69
  338.1 3.2 add_convert_fusion.1
  341.3 20.6 %all_to_all.40 = bf16[8,96,512]{2,1,0:T(8,128)(2,1)S(1)} all-to-all(bf16[8,96,512]{2,1,0:T(8,128)(2,1)S(1)} %get-tuple-element.47), channel_id=1, replica_groups=mesh['dp'=4,'row'=2,'col'=4] {'row','col'}, dimensions={0} | all-to-all | bytes 1572864 | tf_op jit(solution)/shard_map/all_to_all | solution.py:89
  361.9 3.5 all-to-all-start.2
  365.6 17.6 %reduce-scatter.5.cloned.1.call-done = bf16[1,586,384]{2,1,0:T(8,128)(2,1)} async-done(((bf16[8,586,384]{2,1,0:T(8,128)(2,1)}), bf16[1,586,384]{2,1,0:T(8,128)(2,1)}) %reduce-scatter.5.cloned.1.call-update) | async-done | bytes 450064 | tf_op jit(solution)/shard_map/reduce_scatter | solution.py:205
  383.1 57.8 %reduce-scatter.11.cloned.1.call-done = bf16[1,768,384]{2,1,0:T(8,128)(2,1)} async-done(((bf16[8,768,384]{2,1,0:T(8,128)(2,1)}), bf16[1,768,384]{2,1,0:T(8,128)(2,1)}) %reduce-scatter.11.cloned.1.call-update) | async-done | bytes 589840 | tf_op jit(solution)/shard_map/reduce_scatter | solution.py:205
  441.0 57.4 %reduce-scatter.9.cloned.1.call-done = bf16[1,384,768]{2,1,0:T(8,128)(2,1)} async-done(((bf16[8,384,768]{2,1,0:T(8,128)(2,1)}), bf16[1,384,768]{2,1,0:T(8,128)(2,1)}) %reduce-scatter.9.cloned.1.call-update) | async-done | bytes 589840 | tf_op jit(solution)/shard_map/reduce_scatter | solution.py:205
  499.9 3.5 all-to-all-start.7
  504.9 26.5 %all-to-all-done.7 = bf16[2,8,96,256]{3,1,2,0:T(8,128)(2,1)S(1)} async-done(((bf16[2,8,96,256]{3,1,2,0:T(8,128)(2,1)}), bf16[2,8,96,256]{3,1,2,0:T(8,128)(2,1)S(1)}, u32[]{:S(2)}, u32[]{:S(2)}) %all-to-all-start.7) | async-done | bytes 786464 | tf_op jit(solution)/shard_map/all_to_all | solution.py:91
  531.4 3.5 all-to-all-start.3
  536.2 15.9 %all-to-all-done.3 = bf16[2,8,96,256]{3,1,2,0:T(8,128)(2,1)S(1)} async-done(((bf16[2,8,96,256]{3,1,2,0:T(8,128)(2,1)}), bf16[2,8,96,256]{3,1,2,0:T(8,128)(2,1)S(1)}, u32[]{:S(2)}, u32[]{:S(2)}) %all-to-all-start.3) | async-done | bytes 786464 | tf_op jit(solution)/shard_map/all_to_all | solution.py:91
  553.3 38.6 %all-reduce.8.cloned.1.call-done = (bf16[586,384]{1,0:T(8,128)(2,1)}, bf16[192,384]{1,0:T(8,128)(2,1)}, bf16[384,768]{1,0:T(8,128)(2,1)}, bf16[768,384]{1,0:T(8,128)(2,1)}) async-done(((bf16[586,384]{1,0:T(8,128)(2,1)}, bf16[192,384]{1,0:T(8,128)(2,1)}, bf16[384,768]{1,0:T(8,128)(2,1)}, bf16[768,384]{1,0:T(8,128)(2,1)}), (bf16[586,384]{1,0:T(8,128)(2,1)}, bf16[192,384]{1,0:T(8,128)(2,1)}, ...) | async-done | bytes 1777168 | tf_op jit(solution)/shard_map/psum | solution.py:205
  (251 shorter events, 57.4 us)
Async XLA Ops:
  7.2 31.3 %copy-start = (s32[8,4,4]{0,2,1:T(4,128)S(1)}, s32[8,4,4]{0,2,1:T(4,128)}, u32[]{:S(2)}) copy-start(s32[8,4,4]{0,2,1:T(4,128)} %param.23) | copy-start | bytes 1540
  7.2 6.9 %copy-start.23 = (bf16[96,4096]{1,0:T(8,128)(2,1)S(1)}, bf16[96,4096]{1,0:T(8,128)(2,1)}, u32[]{:S(2)}) copy-start(bf16[96,4096]{1,0:T(8,128)(2,1)} %param.20) | copy-start | bytes 2359300
  7.2 59.8 %all-reduce.6.cloned.1.call-start = ((), (), s32[]{:S(2)}) async-start(), calls=%async_computation.20 | async-start | bytes 237568
  12.0 99.5 %all-gather.10.cloned.1.call-start = ((), (), s32[]{:S(2)}) async-start(), calls=%async_computation.16 | async-start | bytes 3981312 | tf_op jit(solution)/shard_map/all_gather | solution.py:95
  12.8 125.5 %all-gather.12.cloned.1.call-start = ((), (), s32[]{:S(2)}) async-start(), calls=%async_computation.17 | async-start | bytes 1327104 | tf_op jit(solution)/shard_map/all_gather | solution.py:95
  13.5 165.0 %all-gather.14.cloned.1.call-start = ((), (), s32[]{:S(2)}) async-start(), calls=%async_computation.18 | async-start | bytes 5308416 | tf_op jit(solution)/shard_map/all_gather | solution.py:95
  14.3 5.2 copy-start.24
  15.2 15.9 %all-to-all-start = ((bf16[2,8,96,256]{3,1,2,0:T(8,128)(2,1)}), bf16[2,8,96,256]{3,1,2,0:T(8,128)(2,1)S(1)}, u32[]{:S(2)}, u32[]{:S(2)}) async-start(bf16[2,8,96,256]{3,1,2,0:T(8,128)(2,1)} %copy.120), calls=%async_computation | async-start | bytes 1572864 | tf_op jit(solution)/shard_map/all_to_all | solution.py:83
  31.1 14.0 %all-to-all-start.4 = ((bf16[2,8,96,256]{3,1,2,0:T(8,128)(2,1)}), bf16[2,8,96,256]{3,1,2,0:T(8,128)(2,1)S(1)}, u32[]{:S(2)}, u32[]{:S(2)}) async-start(bf16[2,8,96,256]{3,1,2,0:T(8,128)(2,1)} %copy.130), calls=%async_computation.4 | async-start | bytes 1572864 | tf_op jit(solution)/shard_map/all_to_all | solution.py:83
  34.6 184.7 %all-gather.16.cloned.1.call-start = ((), (), s32[]{:S(2)}) async-start(), calls=%async_computation.19 | async-start | bytes 5308416 | tf_op jit(solution)/shard_map/all_gather | solution.py:95
  45.1 28.2 %all-to-all-start.1 = ((bf16[8,96,512]{2,1,0:T(8,128)(2,1)}), bf16[8,96,512]{2,1,0:T(8,128)(2,1)S(1)}, u32[]{:S(2)}, u32[]{:S(2)}) async-start(bf16[8,96,512]{2,1,0:T(8,128)(2,1)} %reshape.770), calls=%async_computation.1 | async-start | bytes 1572864 | tf_op jit(solution)/shard_map/all_to_all | solution.py:85
  69.1 4.1 copy-start.35
  69.4 9.0 %copy-start.46 = (f32[2,384]{1,0:T(2,128)}, f32[2,384]{1,0:T(2,128)S(1)}, u32[]{:S(2)}) copy-start(f32[2,384]{1,0:T(2,128)S(1)} %mul.364) | copy-start | bytes 9220
  73.3 4.8 copy-start.2
  73.3 124.6 %all-to-all-start.5 = ((bf16[8,96,512]{2,1,0:T(8,128)(2,1)}), bf16[8,96,512]{2,1,0:T(8,128)(2,1)}, u32[]{:S(2)}, u32[]{:S(2)}) async-start(bf16[8,96,512]{2,1,0:T(8,128)(2,1)} %reshape.782), calls=%async_computation.5 | async-start | bytes 1572864 | tf_op jit(solution)/shard_map/all_to_all | solution.py:85
  77.5 288.0 %reduce-scatter.7.cloned.1.call-start = ((), (), s32[]{:S(2)}) async-start(), calls=%async_computation.13 | async-start | bytes 1327104 | tf_op jit(solution)/shard_map/reduce_scatter | solution.py:205
  78.4 37.2 %copy-start.44 = (f32[512]{0:T(512)}, f32[512]{0:T(512)S(1)}, u32[]{:S(2)}) copy-start(f32[512]{0:T(512)S(1)} %add_rsqrt_fusion.3) | copy-start | bytes 6148
  78.7 32.8 %copy-start.26 = (bf16[2,384,512,1,1]{2,1,4,3,0:T(8,128)(2,1)}, bf16[2,384,512,1,1]{2,1,4,3,0:T(8,128)(2,1)S(1)}, u32[]{:S(2)}) copy-start(bf16[2,384,512,1,1]{2,1,4,3,0:T(8,128)(2,1)S(1)} %fusion.41) | copy-start | bytes 2359300
  219.3 8.5 %slice-start = ((s8[6291456]{0:T(1024)(128)(4,1)}), s8[4194304]{0:T(1024)(128)(4,1)S(1)}, s32[]{:S(2)}) async-start(s8[6291456]{0:T(1024)(128)(4,1)} %bitcast.284), calls=%async_computation.22 | async-start | bytes 8388608
  219.3 8.5 %slice-start.1 = ((s8[6291456]{0:T(1024)(128)(4,1)}), s8[2097152]{0:T(1024)(128)(4,1)S(1)}, s32[]{:S(2)}) async-start(s8[6291456]{0:T(1024)(128)(4,1)} %bitcast.284), calls=%async_computation.23 | async-start | bytes 4194304
  227.9 7.8 %copy-start.9 = (f32[2,384,512]{2,1,0:T(8,128)S(1)}, f32[2,384,512]{2,1,0:T(8,128)}, u32[]{:S(2)}) copy-start(f32[2,384,512]{2,1,0:T(8,128)} %copy-done.8) | copy-start | bytes 4718596
  235.6 6.1 copy-start.17
  249.3 7.9 %copy-start.19 = (f32[1,4,192,512]{3,2,0,1:T(8,128)S(1)}, f32[1,4,192,512]{3,2,0,1:T(8,128)}, u32[]{:S(2)}) copy-start(f32[1,4,192,512]{3,2,0,1:T(8,128)} %get-tuple-element.46) | copy-start | bytes 4718596
  249.3 7.9 %copy-start.25 = (bf16[768,512]{1,0:T(8,128)(2,1)S(1)}, bf16[768,512]{1,0:T(8,128)(2,1)}, u32[]{:S(2)}) copy-start(bf16[768,512]{1,0:T(8,128)(2,1)} %copy.135) | copy-start | bytes 2359300
  249.3 16.8 %slice-start.2 = ((s8[12582912]{0:T(1024)(128)(4,1)}), s8[4194304]{0:T(1024)(128)(4,1)S(1)}, s32[]{:S(2)}) async-start(s8[12582912]{0:T(1024)(128)(4,1)} %bitcast.297), calls=%async_computation.24 | async-start | bytes 8388608
  249.3 16.8 %slice-start.3 = ((s8[12582912]{0:T(1024)(128)(4,1)}), s8[4194304]{0:T(1024)(128)(4,1)S(1)}, s32[]{:S(2)}) async-start(s8[12582912]{0:T(1024)(128)(4,1)} %bitcast.297), calls=%async_computation.25 | async-start | bytes 8388608
  257.2 8.9 %slice-start.4 = ((s8[12582912]{0:T(1024)(128)(4,1)}), s8[4194304]{0:T(1024)(128)(4,1)S(1)}, s32[]{:S(2)}) async-start(s8[12582912]{0:T(1024)(128)(4,1)} %bitcast.297), calls=%async_computation.26 | async-start | bytes 8388608
  266.1 6.5 %copy-start.15 = (f32[1,4,192,512]{3,2,0,1:T(8,128)S(1)}, f32[1,4,192,512]{3,2,0,1:T(8,128)}, u32[]{:S(2)}) copy-start(f32[1,4,192,512]{3,2,0,1:T(8,128)} %get-tuple-element.45) | copy-start | bytes 4718596
  272.6 2.9 copy-start.13
  279.4 103.8 %reduce-scatter.5.cloned.1.call-start = ((), (), s32[]{:S(2)}) async-start(), calls=%async_computation.12 | async-start | bytes 4091904 | tf_op jit(solution)/shard_map/reduce_scatter | solution.py:205
  288.7 3.8 copy-start.18
  288.8 3.8 copy-start.20
  288.8 3.8 copy-start.27
  298.8 142.2 %reduce-scatter.11.cloned.1.call-start = ((), (), s32[]{:S(2)}) async-start(), calls=%async_computation.15 | async-start | bytes 5308416 | tf_op jit(solution)/shard_map/reduce_scatter | solution.py:205
  312.0 186.3 %reduce-scatter.9.cloned.1.call-start = ((), (), s32[]{:S(2)}) async-start(), calls=%async_computation.14 | async-start | bytes 5308416 | tf_op jit(solution)/shard_map/reduce_scatter | solution.py:205
  332.2 5.8 copy-start.5
  332.2 5.8 copy-start.7
  332.2 5.8 copy-start.14
  332.2 5.8 copy-start.43
  332.2 5.8 copy-start.48
  361.9 137.9 %all-to-all-start.2 = ((bf16[8,96,512]{2,1,0:T(8,128)(2,1)}), bf16[8,96,512]{2,1,0:T(8,128)(2,1)S(1)}, u32[]{:S(2)}, u32[]{:S(2)}) async-start(bf16[8,96,512]{2,1,0:T(8,128)(2,1)} %get-tuple-element.48), calls=%async_computation.2 | async-start | bytes 1572864 | tf_op jit(solution)/shard_map/all_to_all | solution.py:89
  365.5 226.4 %all-reduce.8.cloned.1.call-start = ((), (), s32[]{:S(2)}) async-start(), calls=%async_computation.21 | async-start | bytes 3563520 | tf_op jit(solution)/shard_map/psum | solution.py:205
  499.9 31.5 %all-to-all-start.7 = ((bf16[2,8,96,256]{3,1,2,0:T(8,128)(2,1)}), bf16[2,8,96,256]{3,1,2,0:T(8,128)(2,1)S(1)}, u32[]{:S(2)}, u32[]{:S(2)}) async-start(bf16[2,8,96,256]{3,1,2,0:T(8,128)(2,1)} %copy.140), calls=%async_computation.7 | async-start | bytes 1572864 | tf_op jit(solution)/shard_map/all_to_all | solution.py:91
  531.4 20.7 %all-to-all-start.3 = ((bf16[2,8,96,256]{3,1,2,0:T(8,128)(2,1)}), bf16[2,8,96,256]{3,1,2,0:T(8,128)(2,1)S(1)}, u32[]{:S(2)}, u32[]{:S(2)}) async-start(bf16[2,8,96,256]{3,1,2,0:T(8,128)(2,1)} %copy.128), calls=%async_computation.3 | async-start | bytes 1572864 | tf_op jit(solution)/shard_map/all_to_all | solution.py:91
  591.9 4.7 copy-start.32
  591.9 5.5 copy-start.30
  594.6 3.9 copy-start.29
  597.4 2.8 copy-start.1
  (24 other events, 34.5 us)
Sparse Core Ops, SparseCore 0:
  12.1 54.8 all-reduce.5
  69.1 42.3 all-gather.9
  113.5 24.0 all-gather.11
  139.5 38.9 all-gather.13
  180.4 38.9 all-gather.15
  279.5 36.7 reduce-scatter.6
  319.8 63.2 reduce-scatter.4
  387.0 53.9 reduce-scatter.10
  444.4 53.8 reduce-scatter.8
  501.0 90.8 all-reduce.7
where the time goes:
time: 613 us; the launch traced here: 607 us
  waiting for transfers between devices  337 us (55%)
  matrix products  99.4 us (16%)
  local copies, waits for them, and re-layouts  60.3 us (10%)
  other arithmetic  45 us (7%)
  starting transfers between devices  26.8 us (4%)
  blocking collectives  20.6 us (3%)
  between operations  17.9 us (3%)
    reduce_scatter x4, waiting for transfers between devices, reduce(): lax.psum_scatter(v, RC, scatter_dimension=0, tiled=False)  133 us
    dot_general x17, matrix products, mm(): return jnp.einsum(spec, a, b, preferred_element_type=f32)  88.7 us
    all_gather x4, waiting for transfers between devices, gather(): return lax.all_gather(v, RC, axis=0)  88.3 us
    all_to_all x2, waiting for transfers between devices, from_unit(): v = lax.all_to_all(v, 'dp', 0, 0, axis_index_groups=groups, tiled=True)  42.4 us
    psum x1, waiting for transfers between devices, reduce(): lax.psum(lax.psum_scatter(v, RC, scatter_dimension=0, tiled=False), 'dp')  38.6 us
    unnamed x11, waiting for transfers between devices  20.7 us
    all_to_all x1, blocking collectives, from_unit(): v = lax.all_to_all(v.reshape(n, fl, unit), RC, 0, 0, tiled=True)  20.6 us
    all_to_all x2, waiting for transfers between devices, to_unit(): v = lax.all_to_all(v, 'dp', 0, 0, axis_index_groups=groups, tiled=True)  14.4 us
  transfers between devices with their start and end apart: 17, of which 12 were waited for; matrix products, arithmetic and copies ran while one was open for 21% of the time, Pallas kernels for 0%

commit v1 on v0

--- a/solution.py
+++ b/solution.py
@@ -202,7 +202,9 @@
 
     def reduce(v):
         v = v.reshape((n,) + v.shape[2:])
-        return lax.psum(lax.psum_scatter(v, RC, scatter_dimension=0, tiled=False), "dp")
+        return jnp.sum(
+            lax.all_gather(lax.psum_scatter(v, RC, scatter_dimension=0, tiled=False), "dp"), axis=0
+        )
 
     shr_w_g = reduce(d_shr_w).astype(f32)
     exp_w_g = reduce(d_exp_w).astype(f32)

time: 613 us -> 662 us (1.080)
  waiting for transfers between devices: 337 us -> 383 us
  other arithmetic: 45 us -> 52.1 us
    all_gather x0 -> x3, waiting for transfers between devices: none -> 115 us  [reduce(): lax.all_gather(lax.psum_scatter(v, RC, scatter_dimension=0, tiled=False),...]
    psum x1 -> x0, waiting for transfers between devices: 38.6 us -> none  [reduce(): lax.psum(lax.psum_scatter(v, RC, scatter_dimension=0, tiled=False), 'dp')]
    all_to_all x2, waiting for transfers between devices: 42.4 us -> 18.2 us  [from_unit(): v = lax.all_to_all(v, 'dp', 0, 0, axis_index_groups=groups, tiled=True)]
    all_to_all x1 -> x0, blocking collectives: 20.6 us -> none  [from_unit(): v = lax.all_to_all(v.reshape(n, fl, unit), RC, 0, 0, tiled=True)]
    all_gather x0 -> x1, blocking collectives: none -> 20.6 us  [reduce(): lax.all_gather(lax.psum_scatter(v, RC, scatter_dimension=0, tiled=False),...]
    reduce_scatter x4, waiting for transfers between devices: 133 us -> 116 us  [reduce(): lax.psum_scatter(v, RC, scatter_dimension=0, tiled=False)]
    all_to_all x1 -> x2, waiting for transfers between devices: 0.01 us -> 10.1 us  [from_unit(): v = lax.all_to_all(v.reshape(n, fl, unit), RC, 0, 0, tiled=True)]
    reduce_sum x0 -> x4, other arithmetic: none -> 6.74 us  [reduce(): jnp.sum(lax.all_gather(lax.psum_scatter(v, RC, scatter_dimension=0, tiled...]
  transfers between devices with their start and end apart: 17 -> 20, of which waited for: 12 -> 15; matrix products, arithmetic and copies ran while one was open for 21% -> 18% of each run, Pallas kernels for 0% -> 0%
where the time goes in v1:
time: 662 us; the launch traced here: 656 us
  waiting for transfers between devices  383 us (58%)
  matrix products  93.7 us (14%)
  local copies, waits for them, and re-layouts  57.8 us (9%)
  other arithmetic  52.1 us (8%)
  starting transfers between devices  30.6 us (5%)
  blocking collectives  20.6 us (3%)
  between operations  17.9 us (3%)
    reduce_scatter x4, waiting for transfers between devices, reduce(): lax.psum_scatter(v, RC, scatter_dimension=0, tiled=False)  116 us
    all_gather x3, waiting for transfers between devices, reduce(): lax.all_gather(lax.psum_scatter(v, RC, scatter_dimension=0, tiled=False),...  115 us
    all_gather x4, waiting for transfers between devices, gather(): return lax.all_gather(v, RC, axis=0)  88.5 us
    dot_general x17, matrix products, mm(): return jnp.einsum(spec, a, b, preferred_element_type=f32)  82.9 us
    unnamed x13, waiting for transfers between devices  20.7 us
    all_gather x1, blocking collectives, reduce(): lax.all_gather(lax.psum_scatter(v, RC, scatter_dimension=0, tiled=False),...  20.6 us
    all_to_all x2, waiting for transfers between devices, from_unit(): v = lax.all_to_all(v, 'dp', 0, 0, axis_index_groups=groups, tiled=True)  18.2 us
    all_to_all x2, waiting for transfers between devices, to_unit(): v = lax.all_to_all(v, 'dp', 0, 0, axis_index_groups=groups, tiled=True)  14.4 us
  transfers between devices with their start and end apart: 20, of which 15 were waited for; matrix products, arithmetic and copies ran while one was open for 18% of the time, Pallas kernels for 0%

profile of v1, /device:TPU:0, one launch (start us, length us, event | category | flops | bytes accessed | tf_op | source)
XLA Modules:
  0.0 655.8 jit_solution(14088956415204731199)
XLA Ops:
  15.2 4.3 all-to-all-start
  20.6 10.5 %all-to-all-done = bf16[2,8,96,256]{3,1,2,0:T(8,128)(2,1)S(1)} async-done(((bf16[2,8,96,256]{3,1,2,0:T(8,128)(2,1)}), bf16[2,8,96,256]{3,1,2,0:T(8,128)(2,1)S(1)}, u32[]{:S(2)}, u32[]{:S(2)}) %all-to-all-start) | async-done | bytes 786464 | tf_op jit(solution)/shard_map/all_to_all | solution.py:83
  31.1 3.5 all-to-all-start.4
  41.1 4.0 all-to-all-done.4
  45.1 3.5 all-to-all-start.1
  48.9 18.1 %all-reduce.4.cloned.1.call-done = f32[29184]{0:T(1024)} async-done(((f32[29184]{0:T(1024)}), f32[29184]{0:T(1024)}) %all-reduce.4.cloned.1.call-update) | async-done | bytes 116752
  73.6 4.2 all-to-all-start.5
  79.3 31.8 %all-gather.19.cloned.1.call-done = bf16[24,192,384]{2,1,0:T(8,128)(2,1)} async-done(((bf16[3,192,384]{2,1,0:T(8,128)(2,1)}), bf16[24,192,384]{2,1,0:T(8,128)(2,1)}) %all-gather.19.cloned.1.call-update) | async-done | bytes 3538960 | tf_op jit(solution)/shard_map/all_gather | solution.py:95
  111.1 4.1 convolution_bitcast_fusion.1
  117.5 10.8 %fusion.64 = (f32[12,512]{1,0:T(8,128)S(1)}, f32[12,512,512]{2,1,0:T(8,128)}) fusion(pred[512,512]{1,0:T(8,128)(4,1)S(1)} %broadcast_compare_fusion, bf16[12,64,512]{2,1,0:T(8,128)(2,1)S(1)} %bitcast.295, f32[12,64,512]{2,1,0:T(8,128)} %bitcast.298, f32[12,64]{1,0:T(8,128)S(1)} %add.252), kind=kOutput, calls=%fused_computation.139 | convolution fusion | flops 416023040 | bytes 15232000 | tf_op jit(solution)/shard_map/sub | solution.py:148
  128.3 6.6 fusion.65
  142.8 35.3 %all-gather.23.cloned.1.call-done = bf16[3072,768]{1,0:T(8,128)(2,1)} async-done(((bf16[384,768]{1,0:T(8,128)(2,1)}), bf16[3072,768]{1,0:T(8,128)(2,1)}) %all-gather.23.cloned.1.call-update) | async-done | bytes 4718608 | tf_op jit(solution)/shard_map/all_gather | solution.py:95
  178.1 9.2 %fusion.54 = (f32[512]{0:T(512)S(1)}, f32[4,768,512]{1,2,0:T(8,128)}, f32[4,768,512]{1,2,0:T(8,128)}) fusion(f32[4,768]{1,0:T(4,128)S(1)} %get-tuple-element.53, bf16[2,4,384,768]{3,2,1,0:T(8,128)(2,1)} %bitcast.336, f32[2,384]{1,0:T(2,128)S(1)} %add.267, f32[2,384]{1,0:T(2,128)S(1)} %mul.381, f32[512]{0:T(512)S(1)} %add_rsqrt_fusion.1, ...), kind=kOutput, calls=%fused_computation.130 | convolution fusion | flops 2427321856 | bytes 18898944 | tf_op jit(solution)/shard_map/rckn,rkt->cnt/dot_general | solution.py:16
  187.3 6.6 %copy.132 = f32[4,768,512]{2,1,0:T(8,128)} copy(f32[4,768,512]{1,2,0:T(8,128)} %get-tuple-element.75) | data formatting | bytes 12582912 | tf_op jit(solution)/shard_map/rckn,rkt->cnt/dot_general | solution.py:16
  193.9 3.5 multiply_reduce_fusion.2
  197.5 21.4 %all-gather.25.cloned.1.call-done = bf16[6144,384]{1,0:T(8,128)(2,1)} async-done(((bf16[768,384]{1,0:T(8,128)(2,1)}), bf16[6144,384]{1,0:T(8,128)(2,1)}) %all-gather.25.cloned.1.call-update) | async-done | bytes 4718608 | tf_op jit(solution)/shard_map/all_gather | solution.py:95
  218.9 8.5 %fusion.8 = (bf16[3072]{0:T(1024)(128)(2,1)S(1)}, f32[512]{0:T(512)S(1)}, f32[512]{0:T(512)S(1)}, bf16[3072]{0:T(1024)(128)(2,1)S(1)}, f32[3072,512,1]{1,0,2:T(8,128)S(1)}) fusion(f32[4,768,512]{2,1,0:T(8,128)} %copy.132, f32[512]{0:T(512)S(1)} %broadcast_multiply_fusion.2, f32[3072]{0:T(1024)S(1)} %add.280, f32[512]{0:T(512)S(1)} %add_rsqrt_fusion, ...), kind=kOutput, calls=%fused_computation.17 | convolution fusion | flops 2437932032 | bytes 18132992 | tf_op jit(solution)/shard_map/rfd,rdt->ft/dot_general | solution.py:16
  227.5 7.7 %fusion.52 = (bf16[3072]{0:T(1024)(128)(2,1)S(1)}, bf16[3072,512]{1,0:T(8,128)(2,1)S(1)}) fusion(f32[512]{0:T(512)S(1)} %get-tuple-element.85, f32[512]{0:T(512)S(1)} %broadcast_multiply_fusion.2, f32[3072]{0:T(1024)S(1)} %add.280, f32[4,768,512]{2,1,0:T(8,128)S(1)} %bitcast.281, f32[512]{0:T(512)S(1)} %get-tuple-element.86, f32[3072]{0:T(1024)S(1)} %mul.396, ...), kind=kLoop, calls=%fused_computation.129 | loop fusion | flops 31454208 | bytes 15767552 | tf_op jit(solution)/shard_map/reduce_sum | solution.py:175
  235.2 6.0 fusion.30
  247.0 7.1 %fusion.67 = (bf16[12,64]{1,0:T(8,128)(2,1)S(1)}, bf16[12,64,512]{2,1,0:T(8,128)(2,1)S(1)}) fusion(bf16[12,64,512]{2,1,0:T(8,128)(2,1)} %bitcast.327, f32[12,512,512]{2,1,0:T(8,128)} %get-tuple-element.72, f32[12,512]{1,0:T(8,128)S(1)} %get-tuple-element.71), kind=kOutput, calls=%fused_computation.142 | convolution fusion | flops 409730304 | bytes 14181888 | tf_op jit(solution)/shard_map/heq,hkq->hek/dot_general | solution.py:16
  254.1 8.9 %multiply_reduce_fusion = (f32[12,512]{1,0:T(8,128)S(1)}, f32[12,512,512]{2,1,0:T(8,128)}) fusion(f32[12,512,512]{2,1,0:T(8,128)} %get-tuple-element.72, f32[12,512]{1,0:T(8,128)S(1)} %get-tuple-element.71, bf16[12,64,512]{2,1,0:T(8,128)(2,1)S(1)} %bitcast.328, f32[12,64,512]{2,1,0:T(8,128)S(1)} %bitcast.318, f32[12,64]{1,0:T(8,128)S(1)} %add.241), kind=kOutput, calls=%fused_computation.2 | convolution fusion | flops 412870656 | bytes 27577344 | tf_op jit(solution)/shard_map/hek,heq->hkq/dot_general | solution.py:16
  263.0 6.5 multiply_convert_fusion
  273.5 3.3 fusion.22
  276.8 3.5 convolution_convert_fusion
  283.9 3.4 fusion.51
  287.4 4.1 pad_maximum_fusion
  292.3 4.0 add_convert_fusion
  297.9 4.1 convert_bitcast_fusion
  302.0 2.6 copy.145
  304.9 7.4 %convert_bitcast_fusion.1 = bf16[2,4,384,768]{2,3,0,1:T(8,128)(2,1)} fusion(bf16[4,768,512,1]{2,1,3,0:T(8,128)(2,1)} %bitcast.313, f32[2,384,512]{2,1,0:T(8,128)} %copy-done.9, f32[2,384]{1,0:T(2,128)S(1)} %add.267, f32[2,384]{1,0:T(2,128)S(1)} %mul.381, f32[512]{0:T(512)S(1)} %add_rsqrt_fusion.1, f32[512]{0:T(512)S(1)} %broadcast_multiply_fusion.9), kind=kOutput, calls=%fused_computation.30 | convolution fusion | flops 2420244480 | bytes 9447424 | tf_op jit(solution)/shard_map/rkt,cnt->rckn/dot_general | solution.py:16
  312.3 6.7 %copy.143 = bf16[2,4,384,768]{3,2,1,0:T(8,128)(2,1)} copy(bf16[2,4,384,768]{2,3,0,1:T(8,128)(2,1)} %convert_bitcast_fusion.1) | data formatting | bytes 9437184 | tf_op jit(solution)/shard_map/convert_element_type | solution.py:177
  321.9 18.5 %reduce-scatter.5.cloned.1.call-done = bf16[1,586,384]{2,1,0:T(8,128)(2,1)} async-done(((bf16[8,586,384]{2,1,0:T(8,128)(2,1)}), bf16[1,586,384]{2,1,0:T(8,128)(2,1)}) %reduce-scatter.5.cloned.1.call-update) | async-done | bytes 450064 | tf_op jit(solution)/shard_map/reduce_scatter | solution.py:206
  340.5 57.3 %reduce-scatter.11.cloned.1.call-done = bf16[1,768,384]{2,1,0:T(8,128)(2,1)} async-done(((bf16[8,768,384]{2,1,0:T(8,128)(2,1)}), bf16[1,768,384]{2,1,0:T(8,128)(2,1)}) %reduce-scatter.11.cloned.1.call-update) | async-done | bytes 589840 | tf_op jit(solution)/shard_map/reduce_scatter | solution.py:206
  397.8 4.7 copy.126
  402.5 5.7 fusion.69
  408.2 3.4 add_convert_fusion.1
  411.6 3.6 all-to-all-start.6
  415.2 40.7 %reduce-scatter.9.cloned.1.call-done = bf16[1,384,768]{2,1,0:T(8,128)(2,1)} async-done(((bf16[8,384,768]{2,1,0:T(8,128)(2,1)}), bf16[1,384,768]{2,1,0:T(8,128)(2,1)}) %reduce-scatter.9.cloned.1.call-update) | async-done | bytes 589840 | tf_op jit(solution)/shard_map/reduce_scatter | solution.py:206
  455.9 3.6 all-to-all-start.2
  461.0 10.1 %all-to-all-done.2 = bf16[8,96,512]{2,1,0:T(8,128)(2,1)S(1)} async-done(((bf16[8,96,512]{2,1,0:T(8,128)(2,1)}), bf16[8,96,512]{2,1,0:T(8,128)(2,1)S(1)}, u32[]{:S(2)}, u32[]{:S(2)}) %all-to-all-start.2) | async-done | bytes 786464 | tf_op jit(solution)/shard_map/all_to_all | solution.py:89
  471.1 3.5 all-to-all-start.7
  476.1 9.3 %all-to-all-done.7 = bf16[2,8,96,256]{3,1,2,0:T(8,128)(2,1)S(1)} async-done(((bf16[2,8,96,256]{3,1,2,0:T(8,128)(2,1)}), bf16[2,8,96,256]{3,1,2,0:T(8,128)(2,1)S(1)}, u32[]{:S(2)}, u32[]{:S(2)}) %all-to-all-start.7) | async-done | bytes 786464 | tf_op jit(solution)/shard_map/all_to_all | solution.py:91
  485.5 3.5 all-to-all-start.3
  490.3 8.8 %all-to-all-done.3 = bf16[2,8,96,256]{3,1,2,0:T(8,128)(2,1)S(1)} async-done(((bf16[2,8,96,256]{3,1,2,0:T(8,128)(2,1)}), bf16[2,8,96,256]{3,1,2,0:T(8,128)(2,1)S(1)}, u32[]{:S(2)}, u32[]{:S(2)}) %all-to-all-start.3) | async-done | bytes 786464 | tf_op jit(solution)/shard_map/all_to_all | solution.py:91
  500.3 20.6 %all_gather.53 = bf16[4,192,384]{2,1,0:T(8,128)(2,1)S(1)} all-gather(bf16[1,192,384]{2,1,0:T(8,128)(2,1)} %reduce-scatter.7.cloned.1.call-done), channel_id=1, replica_groups=mesh['dp'=4,'row'=2,'col'=4] {'dp'}, dimensions={0}, use_global_device_ids=true | all-gather | bytes 737280 | tf_op jit(solution)/shard_map/all_gather | solution.py:206
  521.8 22.3 %all-gather.13.cloned.1.call-done = bf16[4,586,384]{2,1,0:T(8,128)(2,1)} async-done(((bf16[1,586,384]{2,1,0:T(8,128)(2,1)}), bf16[4,586,384]{2,1,0:T(8,128)(2,1)}) %all-gather.13.cloned.1.call-update) | async-done | bytes 1800208 | tf_op jit(solution)/shard_map/all_gather | solution.py:206
  549.5 45.0 %all-gather.17.cloned.1.call-done = bf16[4,768,384]{2,1,0:T(8,128)(2,1)} async-done(((bf16[1,768,384]{2,1,0:T(8,128)(2,1)}), bf16[4,768,384]{2,1,0:T(8,128)(2,1)}) %all-gather.17.cloned.1.call-update) | async-done | bytes 2359312 | tf_op jit(solution)/shard_map/all_gather | solution.py:206
  597.9 47.4 %all-gather.15.cloned.1.call-done = bf16[4,384,768]{2,1,0:T(8,128)(2,1)} async-done(((bf16[1,384,768]{2,1,0:T(8,128)(2,1)}), bf16[4,384,768]{2,1,0:T(8,128)(2,1)}) %all-gather.15.cloned.1.call-update) | async-done | bytes 2359312 | tf_op jit(solution)/shard_map/all_gather | solution.py:206
  (257 shorter events, 68.8 us)
Async XLA Ops:
  7.2 31.3 %copy-start = (s32[8,4,4]{0,2,1:T(4,128)S(1)}, s32[8,4,4]{0,2,1:T(4,128)}, u32[]{:S(2)}) copy-start(s32[8,4,4]{0,2,1:T(4,128)} %param.23) | copy-start | bytes 1540
  7.2 6.9 %copy-start.19 = (bf16[96,4096]{1,0:T(8,128)(2,1)S(1)}, bf16[96,4096]{1,0:T(8,128)(2,1)}, u32[]{:S(2)}) copy-start(bf16[96,4096]{1,0:T(8,128)(2,1)} %param.20) | copy-start | bytes 2359300
  7.2 59.8 %all-reduce.4.cloned.1.call-start = ((), (), s32[]{:S(2)}) async-start(), calls=%async_computation.23 | async-start | bytes 237568
  12.0 99.1 %all-gather.19.cloned.1.call-start = ((), (), s32[]{:S(2)}) async-start(), calls=%async_computation.19 | async-start | bytes 3981312 | tf_op jit(solution)/shard_map/all_gather | solution.py:95
  12.8 125.2 %all-gather.21.cloned.1.call-start = ((), (), s32[]{:S(2)}) async-start(), calls=%async_computation.20 | async-start | bytes 1327104 | tf_op jit(solution)/shard_map/all_gather | solution.py:95
  13.5 164.6 %all-gather.23.cloned.1.call-start = ((), (), s32[]{:S(2)}) async-start(), calls=%async_computation.21 | async-start | bytes 5308416 | tf_op jit(solution)/shard_map/all_gather | solution.py:95
  14.3 5.2 copy-start.20
  15.2 15.9 %all-to-all-start = ((bf16[2,8,96,256]{3,1,2,0:T(8,128)(2,1)}), bf16[2,8,96,256]{3,1,2,0:T(8,128)(2,1)S(1)}, u32[]{:S(2)}, u32[]{:S(2)}) async-start(bf16[2,8,96,256]{3,1,2,0:T(8,128)(2,1)} %copy.120), calls=%async_computation | async-start | bytes 1572864 | tf_op jit(solution)/shard_map/all_to_all | solution.py:83
  31.1 14.0 %all-to-all-start.4 = ((bf16[2,8,96,256]{3,1,2,0:T(8,128)(2,1)}), bf16[2,8,96,256]{3,1,2,0:T(8,128)(2,1)S(1)}, u32[]{:S(2)}, u32[]{:S(2)}) async-start(bf16[2,8,96,256]{3,1,2,0:T(8,128)(2,1)} %copy.130), calls=%async_computation.4 | async-start | bytes 1572864 | tf_op jit(solution)/shard_map/all_to_all | solution.py:83
  34.6 184.3 %all-gather.25.cloned.1.call-start = ((), (), s32[]{:S(2)}) async-start(), calls=%async_computation.22 | async-start | bytes 5308416 | tf_op jit(solution)/shard_map/all_gather | solution.py:95
  45.1 28.4 %all-to-all-start.1 = ((bf16[8,96,512]{2,1,0:T(8,128)(2,1)}), bf16[8,96,512]{2,1,0:T(8,128)(2,1)S(1)}, u32[]{:S(2)}, u32[]{:S(2)}) async-start(bf16[8,96,512]{2,1,0:T(8,128)(2,1)} %reshape.770), calls=%async_computation.1 | async-start | bytes 1572864 | tf_op jit(solution)/shard_map/all_to_all | solution.py:85
  68.1 5.5 copy-start.27
  69.4 4.1 copy-start.29
  69.7 9.1 %copy-start.42 = (f32[2,384]{1,0:T(2,128)}, f32[2,384]{1,0:T(2,128)S(1)}, u32[]{:S(2)}) copy-start(f32[2,384]{1,0:T(2,128)S(1)} %mul.364) | copy-start | bytes 9220
  73.6 4.9 copy-start.2
  73.6 123.9 %all-to-all-start.5 = ((bf16[8,96,512]{2,1,0:T(8,128)(2,1)}), bf16[8,96,512]{2,1,0:T(8,128)(2,1)}, u32[]{:S(2)}, u32[]{:S(2)}) async-start(bf16[8,96,512]{2,1,0:T(8,128)(2,1)} %reshape.782), calls=%async_computation.5 | async-start | bytes 1572864 | tf_op jit(solution)/shard_map/all_to_all | solution.py:85
  77.8 262.6 %reduce-scatter.5.cloned.1.call-start = ((), (), s32[]{:S(2)}) async-start(), calls=%async_computation.12 | async-start | bytes 4091904 | tf_op jit(solution)/shard_map/reduce_scatter | solution.py:206
  78.2 62.0 %copy-start.4 = (f32[8,96,512]{2,1,0:T(8,128)}, f32[8,96,512]{2,1,0:T(8,128)S(1)}, u32[]{:S(2)}) copy-start(f32[8,96,512]{2,1,0:T(8,128)S(1)} %convert_element_type.170) | copy-start | bytes 4718596
  78.7 36.5 %copy-start.40 = (f32[512]{0:T(512)}, f32[512]{0:T(512)S(1)}, u32[]{:S(2)}) copy-start(f32[512]{0:T(512)S(1)} %add_rsqrt_fusion.3) | copy-start | bytes 6148
  79.3 31.8 %copy-start.22 = (bf16[2,384,512,1,1]{2,1,4,3,0:T(8,128)(2,1)}, bf16[2,384,512,1,1]{2,1,4,3,0:T(8,128)(2,1)S(1)}, u32[]{:S(2)}) copy-start(bf16[2,384,512,1,1]{2,1,4,3,0:T(8,128)(2,1)S(1)} %fusion.41) | copy-start | bytes 2359300
  218.9 8.5 %slice-start = ((s8[6291456]{0:T(1024)(128)(4,1)}), s8[4194304]{0:T(1024)(128)(4,1)S(1)}, s32[]{:S(2)}) async-start(s8[6291456]{0:T(1024)(128)(4,1)} %bitcast.280), calls=%async_computation.24 | async-start | bytes 8388608
  218.9 8.5 %slice-start.1 = ((s8[6291456]{0:T(1024)(128)(4,1)}), s8[2097152]{0:T(1024)(128)(4,1)S(1)}, s32[]{:S(2)}) async-start(s8[6291456]{0:T(1024)(128)(4,1)} %bitcast.280), calls=%async_computation.25 | async-start | bytes 4194304
  227.5 7.7 %copy-start.10 = (f32[2,384,512]{2,1,0:T(8,128)S(1)}, f32[2,384,512]{2,1,0:T(8,128)}, u32[]{:S(2)}) copy-start(f32[2,384,512]{2,1,0:T(8,128)} %copy-done.9) | copy-start | bytes 4718596
  235.2 6.1 copy-start.17
  246.9 7.1 %copy-start.18 = (f32[1,4,192,512]{3,2,0,1:T(8,128)S(1)}, f32[1,4,192,512]{3,2,0,1:T(8,128)}, u32[]{:S(2)}) copy-start(f32[1,4,192,512]{3,2,0,1:T(8,128)} %get-tuple-element.42) | copy-start | bytes 4718596
  247.0 7.1 %copy-start.21 = (bf16[768,512]{1,0:T(8,128)(2,1)S(1)}, bf16[768,512]{1,0:T(8,128)(2,1)}, u32[]{:S(2)}) copy-start(bf16[768,512]{1,0:T(8,128)(2,1)} %copy.135) | copy-start | bytes 2359300
  247.0 16.0 %slice-start.2 = ((s8[12582912]{0:T(1024)(128)(4,1)}), s8[4194304]{0:T(1024)(128)(4,1)S(1)}, s32[]{:S(2)}) async-start(s8[12582912]{0:T(1024)(128)(4,1)} %bitcast.293), calls=%async_computation.26 | async-start | bytes 8388608
  247.0 16.0 %slice-start.3 = ((s8[12582912]{0:T(1024)(128)(4,1)}), s8[4194304]{0:T(1024)(128)(4,1)S(1)}, s32[]{:S(2)}) async-start(s8[12582912]{0:T(1024)(128)(4,1)} %bitcast.293), calls=%async_computation.27 | async-start | bytes 8388608
  254.1 8.9 %slice-start.4 = ((s8[12582912]{0:T(1024)(128)(4,1)}), s8[4194304]{0:T(1024)(128)(4,1)S(1)}, s32[]{:S(2)}) async-start(s8[12582912]{0:T(1024)(128)(4,1)} %bitcast.293), calls=%async_computation.28 | async-start | bytes 8388608
  263.0 6.5 copy-start.15
  276.8 4.2 copy-start.34
  276.8 4.2 copy-start.41
  276.8 4.2 copy-start.43
  291.6 106.2 %reduce-scatter.11.cloned.1.call-start = ((), (), s32[]{:S(2)}) async-start(), calls=%async_computation.17 | async-start | bytes 5308416 | tf_op jit(solution)/shard_map/reduce_scatter | solution.py:206
  304.7 151.2 %reduce-scatter.9.cloned.1.call-start = ((), (), s32[]{:S(2)}) async-start(), calls=%async_computation.15 | async-start | bytes 5308416 | tf_op jit(solution)/shard_map/reduce_scatter | solution.py:206
  319.0 181.3 %reduce-scatter.7.cloned.1.call-start = ((), (), s32[]{:S(2)}) async-start(), calls=%async_computation.14 | async-start | bytes 1327104 | tf_op jit(solution)/shard_map/reduce_scatter | solution.py:206
  321.9 222.2 %all-gather.13.cloned.1.call-start = ((), (), s32[]{:S(2)}) async-start(), calls=%async_computation.13 | async-start | bytes 2273280 | tf_op jit(solution)/shard_map/all_gather | solution.py:206
  340.5 254.0 %all-gather.17.cloned.1.call-start = ((), (), s32[]{:S(2)}) async-start(), calls=%async_computation.18 | async-start | bytes 2949120 | tf_op jit(solution)/shard_map/all_gather | solution.py:206
  402.5 5.7 copy-start.6
  402.5 5.7 copy-start.8
  402.5 5.7 copy-start.14
  402.5 5.7 copy-start.37
  402.5 5.7 copy-start.44
  411.6 44.3 %all-to-all-start.6 = ((bf16[8,96,512]{2,1,0:T(8,128)(2,1)}), bf16[8,96,512]{2,1,0:T(8,128)(2,1)S(1)}, u32[]{:S(2)}, u32[]{:S(2)}) async-start(bf16[8,96,512]{2,1,0:T(8,128)(2,1)} %get-tuple-element.43), calls=%async_computation.6 | async-start | bytes 1572864 | tf_op jit(solution)/shard_map/all_to_all | solution.py:89
  415.2 230.1 %all-gather.15.cloned.1.call-start = ((), (), s32[]{:S(2)}) async-start(), calls=%async_computation.16 | async-start | bytes 2949120 | tf_op jit(solution)/shard_map/all_gather | solution.py:206
  455.9 15.1 %all-to-all-start.2 = ((bf16[8,96,512]{2,1,0:T(8,128)(2,1)}), bf16[8,96,512]{2,1,0:T(8,128)(2,1)S(1)}, u32[]{:S(2)}, u32[]{:S(2)}) async-start(bf16[8,96,512]{2,1,0:T(8,128)(2,1)} %get-tuple-element.44), calls=%async_computation.2 | async-start | bytes 1572864 | tf_op jit(solution)/shard_map/all_to_all | solution.py:89
  471.1 14.4 %all-to-all-start.7 = ((bf16[2,8,96,256]{3,1,2,0:T(8,128)(2,1)}), bf16[2,8,96,256]{3,1,2,0:T(8,128)(2,1)S(1)}, u32[]{:S(2)}, u32[]{:S(2)}) async-start(bf16[2,8,96,256]{3,1,2,0:T(8,128)(2,1)} %copy.140), calls=%async_computation.7 | async-start | bytes 1572864 | tf_op jit(solution)/shard_map/all_to_all | solution.py:91
  485.5 13.6 %all-to-all-start.3 = ((bf16[2,8,96,256]{3,1,2,0:T(8,128)(2,1)}), bf16[2,8,96,256]{3,1,2,0:T(8,128)(2,1)S(1)}, u32[]{:S(2)}, u32[]{:S(2)}) async-start(bf16[2,8,96,256]{3,1,2,0:T(8,128)(2,1)} %copy.128), calls=%async_computation.3 | async-start | bytes 1572864 | tf_op jit(solution)/shard_map/all_to_all | solution.py:91
  (24 other events, 39.2 us)
Sparse Core Ops, SparseCore 0:
  12.1 54.8 all-reduce.3
  69.1 41.9 all-gather.18
  113.1 24.0 all-gather.20
  139.1 38.9 all-gather.22
  180.0 38.9 all-gather.24
  291.7 48.7 reduce-scatter.4
  343.9 53.8 reduce-scatter.10
  401.6 54.2 reduce-scatter.8
  459.7 36.7 reduce-scatter.6
  498.0 45.9 all-gather.12
  545.7 48.7 all-gather.16
  596.0 49.2 all-gather.14
